TPU v7x, 256 devices: a whole 4x4x8 slice. The times are simulated.
256 devices in a mesh: dp: 32 (over y, x, z_lo), tensor: 8 (over z_hi, core).
Axes of the slice: x: 4, y: 4, z: 8 (z_hi: 4, z_lo: 2; z = z_hi * 2 + z_lo), core: 2. Of those that a mesh axis runs over, the one named last changes fastest.
Arguments:
- grad_out: bfloat16 [24576, 4096], P(('dp', 'tensor')), may hold values from -0.15625 to 0.15625
- activations: bfloat16 [24576, 14336], P('dp', 'tensor'), may hold values from -6 to 6
- grad_dither: float32 [24576, 4096], P(('dp', 'tensor')), may hold values from -0.5 to 0.5
- hidden_dither: float32 [32, 14336], P('dp', 'tensor'), may hold values from -0.25 to 0.25
- feature_dither: float32 [32, 4096], P('dp'), may hold values from -0.25 to 0.25
Outputs:
- weight_grad: float32 [4096, 14336], P('dp', 'tensor')
All inputs are finite; a program needn't handle non-finite values.
Results may differ from a plain program's by a relative error of at most 0.014.
Values may be sent and summed in bfloat16 or wider, within the bound.
A program may use at most 128 MiB of HBM per device.

v0:
```python
import jax
import jax.numpy as jnp
from jax import lax
from jax.sharding import PartitionSpec as P

BLOCK = 128
Y_LEVELS = 8
W_LEVELS = 7
ROW_TILE = 512
epsilon = 1e-06


def decode_rows(code_rows, scale_rows):
    row_total = code_rows.shape[0]
    block_count = code_rows.shape[1] // BLOCK
    held = lax.optimization_barrier(code_rows).astype(jnp.float32)
    values = (
        held.reshape(row_total, block_count, BLOCK) * scale_rows.astype(jnp.float32)[:, :, None]
    )
    return values.reshape(row_total, block_count * BLOCK).astype(jnp.bfloat16)


def decode_terms(code_block, block_scale):
    feat_rows, unit_cols = code_block.shape
    block_count = feat_rows // BLOCK
    held = lax.optimization_barrier(code_block).astype(jnp.float32)
    values = (
        held.reshape(block_count, BLOCK, unit_cols) * block_scale.astype(jnp.float32)[:, None, :]
    )
    return values.reshape(feat_rows, unit_cols).astype(jnp.bfloat16)


def quantize(partial_value, feature_part, hidden_part):
    feat_rows, unit_cols = partial_value.shape
    block_count = feat_rows // BLOCK
    blocks = partial_value.reshape(block_count, BLOCK, unit_cols)
    magnitude = jnp.max(jnp.abs(blocks), axis=1)
    block_scale = ((magnitude + epsilon) / W_LEVELS).astype(jnp.bfloat16)
    scaled = (blocks / block_scale.astype(jnp.float32)[:, None, :]).reshape(feat_rows, unit_cols)
    code_block = (scaled + hidden_part[None, :] + feature_part[:, None]).astype(jnp.bfloat16)
    return (code_block, block_scale)


def per_device(grad_out, activations, grad_dither, hidden_dither, feature_dither):
    row_count, feat_width = grad_out.shape
    block_count = feat_width // BLOCK
    grad_float = grad_out.astype(jnp.float32)
    magnitude = jnp.max(jnp.abs(grad_float).reshape(row_count, block_count, BLOCK), axis=2)
    y_scale = ((magnitude + epsilon) / Y_LEVELS).astype(jnp.bfloat16)
    scaled = (
        grad_float.reshape(row_count, block_count, BLOCK) / y_scale.astype(jnp.float32)[:, :, None]
    )
    y_code = (scaled.reshape(row_count, feat_width) + grad_dither).astype(jnp.bfloat16)
    code_rows, scale_rows = (
        lax.all_gather(y_code, "tensor", axis=0, tiled=True),
        lax.all_gather(y_scale, "tensor", axis=0, tiled=True),
    )
    y_hat = decode_rows(code_rows, scale_rows)
    unit_count = activations.shape[1]
    owners = lax.axis_size("dp")
    own_rows = feat_width // owners
    hidden_noise = hidden_dither[0]
    feature_noise = feature_dither[0]

    def feature_tile(tile_start):
        feat_cols = lax.dynamic_slice_in_dim(y_hat, tile_start, ROW_TILE, 1)
        partial_value = lax.dot_general(
            feat_cols, activations, (((0,), (0,)), ((), ())), preferred_element_type=jnp.float32
        )
        feature_part = lax.dynamic_slice_in_dim(feature_noise, tile_start, ROW_TILE, 0)
        return quantize(partial_value, feature_part, hidden_noise)

    tile_starts = jnp.arange(feat_width // ROW_TILE, dtype=jnp.int32) * ROW_TILE
    code_tiles, scale_tiles = lax.map(feature_tile, tile_starts)
    all_codes = code_tiles.reshape(feat_width, unit_count)
    all_scales = scale_tiles.reshape(block_count, unit_count)
    code_part = lax.all_to_all(all_codes, "dp", split_axis=0, concat_axis=0, tiled=True)
    scale_part = lax.all_to_all(all_scales, "dp", split_axis=0, concat_axis=0, tiled=True)
    unit_cols = code_part.shape[1]
    terms = decode_terms(code_part, scale_part)
    held = lax.optimization_barrier(terms).astype(jnp.float32).reshape(owners, own_rows, unit_cols)
    return jnp.sum(held, axis=0)


def solution(mesh):
    placed = (
        P(("dp", "tensor"), None),
        P("dp", "tensor"),
        P(("dp", "tensor"), None),
        P("dp", "tensor"),
        P("dp", None),
    )
    return jax.shard_map(
        per_device, mesh=mesh, in_specs=placed, out_specs=P("dp", "tensor"), check_vma=False
    )
```

profile of v0, /device:TPU:46, one launch (start us, length us, event | category | flops | bytes accessed | tf_op | source)
XLA Modules:
  0.0 479.5 jit_solution(6907904781474757774)
XLA Ops:
  9.2 3.4 fusion.11
  12.7 17.3 %all-gather = bf16[8,96,32]{1,2,0:T(8,128)(2,1)S(1)} all-gather(bf16[1,96,32]{1,2,0:T(8,128)(2,1)S(1)} %copy.11), channel_id=1, replica_groups=mesh['dp'=32,'tensor'=8] {'tensor'}, dimensions={0}, use_global_device_ids=true | all-gather | bytes 55296 | tf_op jit(solution)/shard_map/all_gather | solution.py:56
  30.1 54.8 %all-gather.3.cloned.1.call-done = bf16[768,4096]{1,0:T(8,128)(2,1)} async-done(((bf16[96,4096]{1,0:T(8,128)(2,1)}), bf16[768,4096]{1,0:T(8,128)(2,1)}) %all-gather.3.cloned.1.call-update) | async-done | bytes 6291472 | tf_op jit(solution)/shard_map/all_gather | solution.py:55
  84.9 7.1 %mul.31 = f32[768,32,128]{2,1,0:T(8,128)} broadcast(f32[768,32]{1,0:T(8,128)S(1)} %bitcast.57), dimensions={0,1} | broadcast | bytes 12681216 | tf_op jit(solution)/shard_map/mul | solution.py:18
  92.0 16.8 %fusion.8 = bf16[768,4096]{1,0:T(8,128)(2,1)} fusion(f32[96,8,32,128]{3,2,1,0:T(8,128)} %bitcast.53, bf16[768,4096]{1,0:T(8,128)(2,1)} %all-gather.3.cloned.1.call-done), kind=kLoop, calls=%fused_computation.16 | loop fusion | flops 9437184 | bytes 25165824 | tf_op jit(solution)/shard_map/convert_element_type | solution.py:20
  108.9 65.0 %while.12 = (s32[]{:T(128)}, bf16[8,512,1792]{2,1,0:T(8,128)(2,1)}, bf16[8,4,1792]{2,1,0:T(4,128)(2,1)S(1)}, s32[8]{0:T(128)S(1)}, bf16[768,4096]{1,0:T(8,128)(2...) while((s32[]{:T(128)}, bf16[8,512,1792]{2,1,0:T(8,128)(2,1)}, ...), condition=%wide.region_3.4_spmd, body=%wide.region_1.3_spmd.sunk | while | flops 1414834176 | bytes 12899519 | solution.py:74
  112.2 3.0 bitcast_reduce_fusion.2
  115.3 1.7 bitcast_dynamic-update-slice_fusion.4
  120.3 3.0 bitcast_reduce_fusion.2
  128.4 3.0 bitcast_reduce_fusion.2
  131.5 1.7 bitcast_dynamic-update-slice_fusion.4
  136.6 3.0 bitcast_reduce_fusion.2
  139.6 1.8 bitcast_dynamic-update-slice_fusion.4
  144.7 3.0 bitcast_reduce_fusion.2
  147.8 1.8 bitcast_dynamic-update-slice_fusion.4
  152.9 3.0 bitcast_reduce_fusion.2
  161.0 3.0 bitcast_reduce_fusion.2
  169.1 2.9 bitcast_reduce_fusion.2
  172.1 1.7 bitcast_dynamic-update-slice_fusion.4
  175.8 13.3 %all_to_all.22 = bf16[32,2,896]{2,1,0:T(2,128)(2,1)S(1)} all-to-all(bf16[32,2,896]{2,1,0:T(2,128)(2,1)S(1)} %reshape.72), channel_id=1, replica_groups=mesh['dp'=32,'tensor'=8] {'dp'}, dimensions={0} | all-to-all | bytes 229376 | tf_op jit(solution)/shard_map/all_to_all | solution.py:78
  189.1 8.4 %all-to-all-start = ((bf16[32,128,1792]{2,1,0:T(8,128)(2,1)}), bf16[32,128,1792]{2,1,0:T(8,128)(2,1)}, u32[]{:S(2)}, u32[]{:S(2)}) async-start(bf16[32,128,1792]{2,1,0:T(8,128)(2,1)} %bitcast.54), calls=%async_computation | async-start | bytes 29360128 | tf_op jit(solution)/shard_map/all_to_all | solution.py:77
  197.7 252.4 %all-to-all-done = bf16[32,128,1792]{2,1,0:T(8,128)(2,1)} async-done(((bf16[32,128,1792]{2,1,0:T(8,128)(2,1)}), bf16[32,128,1792]{2,1,0:T(8,128)(2,1)}, u32[]{:S(2)}, u32[]{:S(2)}) %all-to-all-start) | async-done | bytes 14680096 | tf_op jit(solution)/shard_map/all_to_all | solution.py:77
  450.1 14.1 %fusion.7 = bf16[4096,1792]{1,0:T(8,128)(2,1)} fusion(bf16[4096,1792]{1,0:T(8,128)(2,1)} %bitcast.9, f32[32,1792]{1,0:T(8,128)S(1)} %bitcast.58), kind=kLoop, calls=%fused_computation.14 | loop fusion | flops 22020096 | bytes 29589504 | tf_op jit(solution)/shard_map/convert_element_type | solution.py:30
  464.2 8.5 %convert_reduce_fusion = f32[128,1792]{1,0:T(8,128)} fusion(bf16[32,128,1792]{2,1,0:T(8,128)(2,1)} %bitcast.52), kind=kLoop, calls=%fused_computation.12 | loop fusion | flops 14450688 | bytes 15597568 | tf_op jit(solution)/shard_map/reduce_sum | solution.py:82
  (67 shorter events, 21.3 us)
Async XLA Ops:
  6.5 2.6 copy-start.1
  6.5 78.4 %all-gather.3.cloned.1.call-start = ((), (), s32[]{:S(2)}) async-start(), calls=%async_computation.2 | async-start | bytes 7077888 | tf_op jit(solution)/shard_map/all_gather | solution.py:55
  92.0 16.8 %copy-start = (bf16[768,1792]{1,0:T(8,128)(2,1)S(1)}, bf16[768,1792]{1,0:T(8,128)(2,1)}, u32[]{:S(2)}) copy-start(bf16[768,1792]{1,0:T(8,128)(2,1)} %param.8) | copy-start | bytes 8257540
  92.0 16.8 %copy-start.2 = (f32[1,1792]{1,0:T(1,128)S(1)}, f32[1,1792]{1,0:T(1,128)}, u32[]{:S(2)}) copy-start(f32[1,1792]{1,0:T(1,128)} %param.10) | copy-start | bytes 21508
  189.1 261.0 %all-to-all-start = ((bf16[32,128,1792]{2,1,0:T(8,128)(2,1)}), bf16[32,128,1792]{2,1,0:T(8,128)(2,1)}, u32[]{:S(2)}, u32[]{:S(2)}) async-start(bf16[32,128,1792]{2,1,0:T(8,128)(2,1)} %bitcast.54), calls=%async_computation | async-start | bytes 29360128 | tf_op jit(solution)/shard_map/all_to_all | solution.py:77
Sparse Core Ops, SparseCore 0:
  12.7 72.1 all-gather.2
where the time goes:
time: 481 us; the launch traced here: 480 us
  waiting for transfers between devices  307 us (64%)
  other arithmetic  60.4 us (13%)
  blocking collectives  30.6 us (6%)
  matrix products  23.9 us (5%)
  local copies, waits for them, and re-layouts  19.7 us (4%)
  loops' own time  15.7 us (3%)
  between operations  13.5 us (3%)
  starting transfers between devices  8.43 us (2%)
    all_to_all x1, waiting for transfers between devices, per_device(): lax.all_to_all(all_codes, 'dp', split_axis=0, concat_axis=0, tiled=True)  252 us
    all_gather x1, waiting for transfers between devices, per_device(): lax.all_gather(y_code, 'tensor', axis=0, tiled=True)  54.8 us
    dot_general x8, matrix products, feature_tile(): lax.dot_general(feat_cols, activations, (((0,), (0,)), ((), ())), preferr...  23.9 us
    all_gather x1, blocking collectives, per_device(): lax.all_gather(y_scale, 'tensor', axis=0, tiled=True)  17.3 us
    convert_element_type x1, other arithmetic, decode_rows(): return values.reshape(row_total, block_count * BLOCK).astype(jnp.bfloat16)  16.8 us
    another operation x1, loops' own time, per_device(): code_tiles, scale_tiles = lax.map(feature_tile, tile_starts)  15.7 us
    dynamic_update_slice x16, other arithmetic, per_device(): code_tiles, scale_tiles = lax.map(feature_tile, tile_starts)  14.2 us
    convert_element_type x1, other arithmetic, decode_terms(): return values.reshape(feat_rows, unit_cols).astype(jnp.bfloat16)  14.1 us
  transfers between devices with their start and end apart: 2, of which 2 were waited for; matrix products, arithmetic and copies ran while one was open for 0% of the time, Pallas kernels for 0%

commit v1 on v0

--- a/solution.py
+++ b/solution.py
@@ -52,7 +52,9 @@
     )
     y_code = (scaled.reshape(row_count, feat_width) + grad_dither).astype(jnp.bfloat16)
     code_rows, scale_rows = (
-        lax.all_gather(y_code, "tensor", axis=0, tiled=True),
+        jnp.concatenate(
+            lax.all_to_all(jnp.stack([y_code] * lax.axis_size("tensor")), "tensor", 0, 0), axis=0
+        ),
         lax.all_gather(y_scale, "tensor", axis=0, tiled=True),
     )
     y_hat = decode_rows(code_rows, scale_rows)

time: 481 us -> 553 us (1.15)
  blocking collectives: 30.6 us -> 161 us
  waiting for transfers between devices: 307 us -> 252 us
  between operations: 13.5 us -> 0.11 us
  starting transfers between devices: 8.43 us -> 16 us
    all_gather x1, blocking collectives: 17.3 us -> 147 us  [per_device(): lax.all_gather(y_scale, 'tensor', axis=0, tiled=True)]
    all_gather x1 -> x0, waiting for transfers between devices: 54.8 us -> none  [per_device(): lax.all_gather(y_code, 'tensor', axis=0, tiled=True)]
    all_to_all x0 -> x1, starting transfers between devices: none -> 7.57 us  [per_device(): lax.all_to_all(jnp.stack([y_code] * lax.axis_size('tensor')), 'tensor', 0...]
  transfers between devices with their start and end apart: 2 -> 2, of which waited for: 2 -> 1; matrix products, arithmetic and copies ran while one was open for 0% -> 0% of each run, Pallas kernels for 0% -> 0%
where the time goes in v1:
time: 553 us; the launch traced here: 552 us
  waiting for transfers between devices  252 us (46%)
  blocking collectives  161 us (29%)
  other arithmetic  59.5 us (11%)
  matrix products  23.9 us (4%)
  local copies, waits for them, and re-layouts  23.7 us (4%)
  starting transfers between devices  16 us (3%)
  loops' own time  15.4 us (3%)
    all_to_all x1, waiting for transfers between devices, per_device(): lax.all_to_all(all_codes, 'dp', split_axis=0, concat_axis=0, tiled=True)  252 us
    all_gather x1, blocking collectives, per_device(): lax.all_gather(y_scale, 'tensor', axis=0, tiled=True)  147 us
    dot_general x8, matrix products, feature_tile(): lax.dot_general(feat_cols, activations, (((0,), (0,)), ((), ())), preferr...  23.9 us
    convert_element_type x1, other arithmetic, decode_rows(): return values.reshape(row_total, block_count * BLOCK).astype(jnp.bfloat16)  16.8 us
    another operation x1, loops' own time, per_device(): code_tiles, scale_tiles = lax.map(feature_tile, tile_starts)  15.4 us
    dynamic_update_slice x16, other arithmetic, per_device(): code_tiles, scale_tiles = lax.map(feature_tile, tile_starts)  14.2 us
    convert_element_type x1, other arithmetic, decode_terms(): return values.reshape(feat_rows, unit_cols).astype(jnp.bfloat16)  14.1 us
    all_to_all x1, blocking collectives, per_device(): lax.all_to_all(all_scales, 'dp', split_axis=0, concat_axis=0, tiled=True)  13.8 us
  transfers between devices with their start and end apart: 2, of which 1 were waited for; matrix products, arithmetic and copies ran while one was open for 0% of the time, Pallas kernels for 0%

profile of v1, /device:TPU:46, one launch (start us, length us, event | category | flops | bytes accessed | tf_op | source)
XLA Modules:
  0.0 551.6 jit_solution(15644811520205131575)
XLA Ops:
  2.6 2.5 fusion.11
  5.2 3.3 stack.2
  8.5 7.6 %all-to-all-start = ((bf16[8,96,4096]{2,1,0:T(8,128)(2,1)}), bf16[8,96,4096]{2,1,0:T(8,128)(2,1)}, u32[]{:S(2)}, u32[]{:S(2)}) async-start(bf16[8,96,4096]{2,1,0:T(8,128)(2,1)} %stack.2), calls=%async_computation | async-start | bytes 12582912 | tf_op jit(solution)/shard_map/all_to_all | solution.py:56
  16.2 147.3 %all-gather = bf16[8,96,32]{1,2,0:T(8,128)(2,1)S(1)} all-gather(bf16[1,96,32]{1,2,0:T(8,128)(2,1)S(1)} %copy.11), channel_id=1, replica_groups=mesh['dp'=32,'tensor'=8] {'tensor'}, dimensions={0}, use_global_device_ids=true | all-gather | bytes 55296 | tf_op jit(solution)/shard_map/all_gather | solution.py:58
  163.6 7.3 %mul.31 = f32[768,32,128]{2,1,0:T(8,128)} broadcast(f32[768,32]{1,0:T(8,128)S(1)} %bitcast.58), dimensions={0,1} | broadcast | bytes 12681216 | tf_op jit(solution)/shard_map/mul | solution.py:18
  171.0 16.8 %fusion.8 = bf16[768,4096]{1,0:T(8,128)(2,1)} fusion(f32[96,8,32,128]{3,2,1,0:T(8,128)} %bitcast.54, bf16[768,4096]{1,0:T(8,128)(2,1)} %bitcast.5), kind=kLoop, calls=%fused_computation.16 | loop fusion | flops 9437184 | bytes 25165824 | tf_op jit(solution)/shard_map/convert_element_type | solution.py:20
  187.8 65.1 %while.12 = (s32[]{:T(128)}, bf16[8,512,1792]{2,1,0:T(8,128)(2,1)}, bf16[8,4,1792]{2,1,0:T(4,128)(2,1)S(1)}, s32[8]{0:T(128)S(1)}, bf16[768,4096]{1,0:T(8,128)(2...) while((s32[]{:T(128)}, bf16[8,512,1792]{2,1,0:T(8,128)(2,1)}, ...), condition=%wide.region_3.4_spmd, body=%wide.region_1.3_spmd.sunk | while | flops 1414834176 | bytes 12899519 | solution.py:76
  191.2 3.0 bitcast_reduce_fusion.2
  194.2 1.7 bitcast_dynamic-update-slice_fusion.4
  199.3 3.0 bitcast_reduce_fusion.2
  207.4 3.0 bitcast_reduce_fusion.2
  215.6 3.0 bitcast_reduce_fusion.2
  218.6 1.8 bitcast_dynamic-update-slice_fusion.4
  223.8 3.0 bitcast_reduce_fusion.2
  226.8 1.8 bitcast_dynamic-update-slice_fusion.4
  232.0 3.0 bitcast_reduce_fusion.2
  240.1 3.0 bitcast_reduce_fusion.2
  248.2 2.9 bitcast_reduce_fusion.2
  251.2 1.7 bitcast_dynamic-update-slice_fusion.4
  254.9 13.8 %all_to_all.27 = bf16[32,2,896]{2,1,0:T(2,128)(2,1)S(1)} all-to-all(bf16[32,2,896]{2,1,0:T(2,128)(2,1)S(1)} %reshape.78), channel_id=1, replica_groups=mesh['dp'=32,'tensor'=8] {'dp'}, dimensions={0} | all-to-all | bytes 229376 | tf_op jit(solution)/shard_map/all_to_all | solution.py:80
  268.7 8.4 %all-to-all-start.1 = ((bf16[32,128,1792]{2,1,0:T(8,128)(2,1)}), bf16[32,128,1792]{2,1,0:T(8,128)(2,1)}, u32[]{:S(2)}, u32[]{:S(2)}) async-start(bf16[32,128,1792]{2,1,0:T(8,128)(2,1)} %bitcast.55), calls=%async_computation.1 | async-start | bytes 29360128 | tf_op jit(solution)/shard_map/all_to_all | solution.py:79
  277.3 251.7 %all-to-all-done.1 = bf16[32,128,1792]{2,1,0:T(8,128)(2,1)} async-done(((bf16[32,128,1792]{2,1,0:T(8,128)(2,1)}), bf16[32,128,1792]{2,1,0:T(8,128)(2,1)}, u32[]{:S(2)}, u32[]{:S(2)}) %all-to-all-start.1) | async-done | bytes 14680096 | tf_op jit(solution)/shard_map/all_to_all | solution.py:79
  529.0 14.1 %fusion.7 = bf16[4096,1792]{1,0:T(8,128)(2,1)} fusion(bf16[4096,1792]{1,0:T(8,128)(2,1)} %bitcast.10, f32[32,1792]{1,0:T(8,128)S(1)} %bitcast.59), kind=kLoop, calls=%fused_computation.14 | loop fusion | flops 22020096 | bytes 29589504 | tf_op jit(solution)/shard_map/convert_element_type | solution.py:30
  543.1 8.5 %convert_reduce_fusion = f32[128,1792]{1,0:T(8,128)} fusion(bf16[32,128,1792]{2,1,0:T(8,128)(2,1)} %bitcast.53), kind=kLoop, calls=%fused_computation.12 | loop fusion | flops 14450688 | bytes 15597568 | tf_op jit(solution)/shard_map/reduce_sum | solution.py:84
  (67 shorter events, 23.6 us)
Async XLA Ops:
  0.0 2.6 copy-start.1
  8.5 155.1 %all-to-all-start = ((bf16[8,96,4096]{2,1,0:T(8,128)(2,1)}), bf16[8,96,4096]{2,1,0:T(8,128)(2,1)}, u32[]{:S(2)}, u32[]{:S(2)}) async-start(bf16[8,96,4096]{2,1,0:T(8,128)(2,1)} %stack.2), calls=%async_computation | async-start | bytes 12582912 | tf_op jit(solution)/shard_map/all_to_all | solution.py:56
  171.0 16.8 %copy-start = (bf16[768,1792]{1,0:T(8,128)(2,1)S(1)}, bf16[768,1792]{1,0:T(8,128)(2,1)}, u32[]{:S(2)}) copy-start(bf16[768,1792]{1,0:T(8,128)(2,1)} %param.8) | copy-start | bytes 8257540
  171.0 16.8 %copy-start.2 = (f32[1,1792]{1,0:T(1,128)S(1)}, f32[1,1792]{1,0:T(1,128)}, u32[]{:S(2)}) copy-start(f32[1,1792]{1,0:T(1,128)} %param.10) | copy-start | bytes 21508
  268.7 260.3 %all-to-all-start.1 = ((bf16[32,128,1792]{2,1,0:T(8,128)(2,1)}), bf16[32,128,1792]{2,1,0:T(8,128)(2,1)}, u32[]{:S(2)}, u32[]{:S(2)}) async-start(bf16[32,128,1792]{2,1,0:T(8,128)(2,1)} %bitcast.55), calls=%async_computation.1 | async-start | bytes 29360128 | tf_op jit(solution)/shard_map/all_to_all | solution.py:79
